TPU v7x, 32 devices: a whole 2x2x4 slice. The times are simulated.
32 devices in a mesh: sky: 8 (over z, x), tm: 4 (over y, core).
Axes of the slice: x: 2, y: 2, z: 4, core: 2. Of those that a mesh axis runs over, the one named last changes fastest.
Arguments:
- observed: float32 [4096, 128], P(('sky', 'tm')), may hold values from -12 to 12
- att_partials: bfloat16 [3, 4096, 128], P(None, ('sky', 'tm')), may hold values from -6 to 6
- src_partials: bfloat16 [5, 4096, 128], P(None, ('sky', 'tm')), may hold values from -6 to 6
- src_slot: int32 [4096], P(('sky', 'tm')), may hold values from 0 to 1023
- knot_block: int32 [4096], P(('sky', 'tm')), may hold values from 0 to 255, as said below
- live_count: int32 [32], P(('sky', 'tm')), may hold values from 32 to 128, as said below
- sources: float32 [5, 8192], P(None, 'sky'), may hold values from -6 to 6
- inverses: float32 [5, 5, 8192], P(None, None, 'sky')
- attitude: float32 [3, 4, 4096], P(None, 'tm', 'sky'), may hold values from -6 to 6
- band_coef: float32 [3, 3, 4, 4096], P(None, None, 'tm', 'sky'), may hold values from 0.5 to 4
- extra_diag: float32 [3, 4, 4096], P(None, 'tm', 'sky'), may hold values from 0.05 to 0.5
- band_offsets: int32 [3], replicated, may hold values from 1 to 16, as said below
Outputs:
- sources_out: float32 [5, 8192], P(None, 'sky')
- attitude_out: float32 [3, 4, 4096], P(None, 'tm', 'sky')
Inputs may be any that keep to these rules, and one draw needn't show every extreme that they name: On every device, the crossings name blocks of one holder (knot_block // 32) at most 32 times, and some holder exactly 32 times; dead crossings carry blocks too. `live_count`: some device uses all its crossings. `band_offsets`: Distinct; one of them is 16.
All inputs are finite; a program needn't handle non-finite values.
Results may differ from a plain program's by a relative error of at most 0.0003.
Values sent between devices are 32-bit elements; how exact they have to be, the bound alone decides.
A program may use at most 64 MiB of HBM per device.

v0:
```python
import jax
import jax.numpy as jnp
from jax import lax
from jax.sharding import PartitionSpec as P

ROWS = 128
BLOCK_KNOTS = 16
HW = 16
SWEEPS = 3
ITERS = 2


def padded_2(block, sides, width):
    for axis, dim in sides:
        count = lax.axis_size(axis)
        forward = [(i, i + 1) for i in range(count - 1)]
        forward.append((count - 1, 0))
        backward = [(target, source) for source, target in forward]
        low = lax.ppermute(
            lax.slice_in_dim(block, block.shape[dim] - width, None, axis=dim), axis, forward
        )
        high = lax.ppermute(lax.slice_in_dim(block, 0, width, axis=dim), axis, backward)
        block = jnp.concatenate([low, block, high], axis=dim)
    return block


def from_behind(value, axis, steps):
    count = lax.axis_size(axis)
    initial, last = (max(0, -steps), min(count, count - steps))
    return lax.ppermute(value, axis, [(source, source + steps) for source in range(initial, last)])


def spline_table():
    rows_pos = jnp.arange(ROWS, dtype=jnp.float32)
    moments = 1.5 + (BLOCK_KNOTS - 3) * (rows_pos + 0.5) / ROWS
    knot_pos = jnp.arange(BLOCK_KNOTS, dtype=jnp.float32)
    dist = jnp.abs(moments[:, None] - knot_pos[None, :])
    inner = 2.0 / 3.0 - dist * dist + 0.5 * dist * dist * dist
    rest = 2.0 - dist
    outer = rest * rest * rest / 6.0
    return jnp.where(dist < 1.0, inner, jnp.where(dist < 2.0, outer, 0.0))


def source_term(src_partials, values):
    total = jnp.zeros(src_partials.shape[1:], jnp.float32)
    for component in range(5):
        total = total + src_partials[component].astype(jnp.float32) * values[component][:, None]
    return total


def neighbour_sum(field, band_terms, band_offsets, base, length):
    total = jnp.zeros(band_terms.shape[1:], jnp.float32)
    for band_index in range(band_terms.shape[0]):
        offset = band_offsets[band_index]
        upper = lax.dynamic_slice_in_dim(field, base + offset, length, 1)
        lower = lax.dynamic_slice_in_dim(field, base - offset, length, 1)
        total = total + band_terms[band_index] * (upper + lower)
    return total


def extend(field, width):
    padded = padded_2(field, (("sky", 1),), width)
    inner_end = padded.shape[1] - width
    left_rim = padded[:, :width]
    right_rim = padded[:, inner_end:]
    from_before = from_behind(left_rim, "tm", 1)
    from_after = from_behind(right_rim, "tm", -1)
    position = lax.axis_index("sky")
    left_rim = jnp.where(position == 0, from_before, left_rim)
    right_rim = jnp.where(position == lax.axis_size("sky") - 1, from_after, right_rim)
    return jnp.concatenate([left_rim, padded[:, width:inner_end], right_rim], axis=1)


def per_device(
    observed,
    att_partials,
    src_partials,
    src_slot,
    knot_block,
    live_count,
    sources,
    inverses,
    attitude,
    band_coef,
    extra_diag,
    band_offsets,
):
    spline = spline_table()
    crossings_here = observed.shape[0]
    knots_here = attitude.shape[2]
    blocks_here = knots_here // BLOCK_KNOTS
    sky_count = lax.axis_size("sky")
    capacity = 2 * crossings_here // sky_count
    slots_total = sky_count * capacity
    live_rows = (jnp.arange(crossings_here, dtype=jnp.int32) < live_count[0]).astype(jnp.float32)[
        :, None
    ]
    band_terms = band_coef[:, :, 0, :]
    extra_terms = extra_diag[:, 0, :]
    diagonal = extra_terms + 2.0 * jnp.sum(band_terms, axis=0)
    knots_now = attitude[:, 0, :]
    sources_now = sources
    holder = knot_block // blocks_here
    local_block = knot_block % blocks_here
    matches = (holder[:, None] == jnp.arange(sky_count, dtype=jnp.int32)[None, :]).astype(jnp.int32)
    earlier = jnp.cumsum(matches, axis=0) - matches
    column = holder * capacity + jnp.sum(earlier * matches, axis=1)
    asked = jnp.full((slots_total,), blocks_here, jnp.int32).at[column].set(local_block)
    wanted = lax.all_to_all(asked, "sky", split_axis=0, concat_axis=0, tiled=True)
    for outer_step in range(ITERS):
        spare = jnp.zeros((3, 1, BLOCK_KNOTS), jnp.float32)
        own_blocks = jnp.concatenate(
            [knots_now.reshape(3, blocks_here, BLOCK_KNOTS), spare], axis=1
        )
        served = jnp.take(jnp.transpose(own_blocks, (0, 2, 1)), wanted, axis=2)
        arrived = lax.all_to_all(served, "sky", split_axis=2, concat_axis=2, tiled=True)
        fetched = jnp.transpose(jnp.take(arrived, column, axis=2), (0, 2, 1))
        att_term = jnp.zeros(observed.shape, jnp.float32)
        for axis_index in range(3):
            att_term = att_term + att_partials[axis_index].astype(jnp.float32) * jnp.dot(
                fetched[axis_index], spline.T, precision=lax.Precision.HIGHEST
            )
        src_values = jnp.take(sources_now, src_slot, axis=1)
        resid = (observed - source_term(src_partials, src_values) - att_term) * live_rows
        rhs = jnp.stack(
            [
                jnp.sum(src_partials[component].astype(jnp.float32) * resid, axis=1)
                for component in range(5)
            ]
        )
        local_normal = jnp.zeros(sources_now.shape, jnp.float32).at[:, src_slot].add(rhs)
        normal = lax.psum(local_normal, "tm")
        step = jnp.einsum("klm,lm->km", inverses, normal, precision=lax.Precision.HIGHEST)
        sources_now = sources_now + step
        resid = resid - live_rows * source_term(src_partials, jnp.take(step, src_slot, axis=1))
        grads = jnp.stack(
            [
                jnp.dot(
                    att_partials[axis_index].astype(jnp.float32) * resid,
                    spline,
                    precision=lax.Precision.HIGHEST,
                )
                for axis_index in range(3)
            ]
        )
        outgoing = (
            jnp.zeros((3, BLOCK_KNOTS, slots_total), jnp.float32)
            .at[:, :, column]
            .set(jnp.transpose(grads, (0, 2, 1)))
        )
        returned = lax.all_to_all(outgoing, "sky", split_axis=2, concat_axis=2, tiled=True)
        summed = (
            jnp.zeros((3, BLOCK_KNOTS, blocks_here + 1), jnp.float32).at[:, :, wanted].add(returned)
        )
        knot_grad = jnp.transpose(summed[:, :, :blocks_here], (0, 2, 1)).reshape(3, knots_here)
        delta = knot_grad / diagonal
        for sweep_index in range(SWEEPS - 1):
            widened = extend(delta, HW)
            delta = (
                knot_grad + neighbour_sum(widened, band_terms, band_offsets, HW, knots_here)
            ) / diagonal
        knots_now = knots_now + delta
    return (sources_now, knots_now[:, None, :])


def solution(mesh):
    placed = (
        P(("sky", "tm"), None),
        P(None, ("sky", "tm"), None),
        P(None, ("sky", "tm"), None),
        P(("sky", "tm")),
        P(("sky", "tm")),
        P(("sky", "tm")),
        P(None, "sky"),
        P(None, None, "sky"),
        P(None, "tm", "sky"),
        P(None, None, "tm", "sky"),
        P(None, "tm", "sky"),
        P(),
    )
    return jax.shard_map(
        per_device,
        mesh=mesh,
        in_specs=placed,
        out_specs=(P(None, "sky"), P(None, "tm", "sky")),
        check_vma=False,
    )
```

profile of v0, /device:TPU:1, one launch (start us, length us, event | category | flops | bytes accessed | tf_op | source)
XLA Modules:
  0.0 230.4 jit_solution(7839276913477497021)
XLA Ops:
  0.6 0.7 and_select_fusion
  1.8 1.0 scatter_custom_fusion
  2.8 0.7 all_to_all.22
  3.4 6.3 %all-to-all-start = ((s32[8,32,1]{1,2,0:T(1,128)}), s32[8,32,1]{1,2,0:T(1,128)S(1)}, u32[]{:S(2)}, u32[]{:S(2)}) async-start(s32[8,32,1]{1,2,0:T(1,128)} %bitcast.8), calls=%async_computation | async-start | bytes 8192 | tf_op jit(solution)/shard_map/all_to_all | solution.py:109
  9.8 0.7 compare_and_fusion.2
  10.5 1.4 fusion.182
  19.5 0.7 reduce.7
  20.4 0.8 fusion.176
  21.4 1.0 copy.72
  22.4 0.6 gather_fusion
  23.4 0.8 fusion.175
  24.9 0.7 fusion.177
  26.4 0.9 copy.65
  27.4 3.6 %copy.86 = f32[5,5,1024]{0,1,2:T(8,128)} copy(f32[5,5,1024]{2,1,0:T(8,128)} %param.25) | data formatting | bytes 204800 | tf_op args[7]
  31.6 0.7 reduce.47
  32.3 1.0 gather_fusion.1
  33.7 1.0 reshape.339
  34.7 5.4 %all-to-all-start.1 = ((f32[8,1,1536]{2,1,0:T(1,128)}), f32[8,1,1536]{2,1,0:T(1,128)S(1)}, u32[]{:S(2)}, u32[]{:S(2)}) async-start(f32[8,1,1536]{2,1,0:T(1,128)} %reshape.339), calls=%async_computation.1 | async-start | bytes 98304 | tf_op jit(solution)/shard_map/all_to_all | solution.py:116
  40.2 5.6 %all-to-all-done.1 = f32[8,1,1536]{2,1,0:T(1,128)S(1)} async-done(((f32[8,1,1536]{2,1,0:T(1,128)}), f32[8,1,1536]{2,1,0:T(1,128)S(1)}, u32[]{:S(2)}, u32[]{:S(2)}) %all-to-all-start.1) | async-done | bytes 49184 | tf_op jit(solution)/shard_map/all_to_all | solution.py:116
  46.3 0.8 reduce.48
  47.4 0.8 gather_fusion.2
  49.6 1.1 scatter_custom_fusion.1
  50.7 18.4 %psum.14 = f32[5,1024]{0,1:T(8,128)S(1)} all-reduce(f32[5,1024]{0,1:T(8,128)S(1)} %scatter_custom_fusion.1), channel_id=1, replica_groups=mesh['sky'=8,'tm'=4] {'tm'}, use_global_device_ids=true, to_apply=%region_9.13 | all-reduce | flops 5120 | bytes 40960 | tf_op jit(solution)/shard_map/psum | solution.py:132
  69.1 8.5 %fusion.185 = f32[1024,1,5]{2,1,0:T(1,128)S(1)} fusion(f32[5,1024,1]{0,2,1:T(1,128)S(1)} %bitcast.304, f32[5,5,1024]{0,1,2:T(8,128)} %copy.86), kind=kOutput, calls=%fused_computation.312 | convolution fusion | flops 307200 | bytes 143360 | tf_op jit(solution)/shard_map/klm,lm->km/dot_general | solution.py:133
  80.7 4.3 %scatter_fusion = f32[3,16,256]{1,0,2:T(4,128)S(1)} fusion(f32[3,16,256]{1,0,2:T(4,128)S(1)} %broadcast.97.clone, s32[128]{0:T(128)S(1)} %get-tuple-element.44, f32[128,3,16]{2,1,0:T(4,128)S(1)} %copy.74), kind=kCustom, calls=%fused_computation.10 | custom fusion | bytes 74240 | tf_op jit(solution)/shard_map/scatter | solution.py:149
  85.0 1.0 reshape.341
  86.0 3.5 %all-to-all-start.2 = ((f32[8,1,1536]{2,1,0:T(1,128)}), f32[8,1,1536]{2,1,0:T(1,128)S(1)}, u32[]{:S(2)}, u32[]{:S(2)}) async-start(f32[8,1,1536]{2,1,0:T(1,128)} %reshape.341), calls=%async_computation.2 | async-start | bytes 98304 | tf_op jit(solution)/shard_map/all_to_all | solution.py:151
  89.6 5.6 %all-to-all-done.2 = f32[8,1,1536]{2,1,0:T(1,128)S(1)} async-done(((f32[8,1,1536]{2,1,0:T(1,128)}), f32[8,1,1536]{2,1,0:T(1,128)S(1)}, u32[]{:S(2)}, u32[]{:S(2)}) %all-to-all-start.2) | async-done | bytes 49184 | tf_op jit(solution)/shard_map/all_to_all | solution.py:151
  95.1 0.8 reduce.49
  96.4 8.8 %scatter_fusion.1 = f32[3,16,33]{1,0,2:T(4,128)S(1)} fusion(f32[3,16,33]{1,0,2:T(4,128)S(1)} %broadcast.94.clone, s32[256]{0:T(256)S(1)} %bitcast.316, f32[256,3,16]{2,1,0:T(4,128)S(1)} %bitcast_bitcast_fusion.1), kind=kCustom, calls=%fused_computation.11 | custom fusion | flops 12288 | bytes 148480 | tf_op jit(solution)/shard_map/scatter-add | solution.py:153
  105.7 3.9 %collective-permute-start.2 = (f32[3,16]{1,0:T(4,128)S(1)}, f32[3,16]{1,0:T(4,128)S(1)}, u32[]{:S(2)}, u32[]{:S(2)}) collective-permute-start(f32[3,16]{1,0:T(4,128)S(1)} %get-tuple-element.69), channel_id=1, source_target_pairs={{4,0},{8,4},{12,8},{16,12},{20,16},{24,20},{28,24},{0,28},{5,1},{9... | collective-permute-start | bytes 584 | tf_op jit(solution)/shard_map/ppermute | solution.py:22
  109.6 1.0 collective-permute-done
  110.6 5.5 %collective-permute-start.1 = (f32[3,16]{1,0:T(4,128)S(1)}, f32[3,16]{1,0:T(4,128)S(1)}, u32[]{:S(2)}, u32[]{:S(2)}) collective-permute-start(f32[3,16]{1,0:T(4,128)S(1)} %collective-permute-done), channel_id=1, source_target_pairs={{0,1},{1,2},{2,3},{4,5},{5,6},{6,7},{8,9},{9,10},{10,11},{12,13},{... | collective-permute-start | bytes 584 | tf_op jit(solution)/shard_map/ppermute | solution.py:30
  116.1 1.9 collective-permute-start.3
  118.1 3.0 %collective-permute-done.3 = f32[3,16]{1,0:T(4,128)S(1)} collective-permute-done((f32[3,16]{1,0:T(4,128)S(1)}, f32[3,16]{1,0:T(4,128)S(1)}, u32[]{:S(2)}, u32[]{:S(2)}) %collective-permute-start.3) | collective-permute-done | bytes 224 | tf_op jit(solution)/shard_map/ppermute | solution.py:30
  121.3 4.2 %collective-permute-start.6 = (f32[3,16]{1,0:T(4,128)S(1)}, f32[3,16]{1,0:T(4,128)S(1)}, u32[]{:S(2)}, u32[]{:S(2)}) collective-permute-start(f32[3,16]{1,0:T(4,128)S(1)} %get-tuple-element.67), channel_id=1, source_target_pairs={{4,0},{8,4},{12,8},{16,12},{20,16},{24,20},{28,24},{0,28},{5,1},{9... | collective-permute-start | bytes 584 | tf_op jit(solution)/shard_map/ppermute | solution.py:22
  125.4 1.0 collective-permute-done.4
  126.4 3.1 %collective-permute-start.5 = (f32[3,16]{1,0:T(4,128)S(1)}, f32[3,16]{1,0:T(4,128)S(1)}, u32[]{:S(2)}, u32[]{:S(2)}) collective-permute-start(f32[3,16]{1,0:T(4,128)S(1)} %collective-permute-done.4), channel_id=1, source_target_pairs={{0,1},{1,2},{2,3},{4,5},{5,6},{6,7},{8,9},{9,10},{10,11},{12,13},{... | collective-permute-start | bytes 584 | tf_op jit(solution)/shard_map/ppermute | solution.py:30
  129.5 1.9 collective-permute-start.7
  131.5 3.0 %collective-permute-done.7 = f32[3,16]{1,0:T(4,128)S(1)} collective-permute-done((f32[3,16]{1,0:T(4,128)S(1)}, f32[3,16]{1,0:T(4,128)S(1)}, u32[]{:S(2)}, u32[]{:S(2)}) %collective-permute-start.7) | collective-permute-done | bytes 224 | tf_op jit(solution)/shard_map/ppermute | solution.py:30
  134.8 1.0 gather_fusion.5
  136.1 1.0 reshape.343
  137.1 3.3 %all-to-all-start.3 = ((f32[8,1,1536]{2,1,0:T(1,128)}), f32[8,1,1536]{2,1,0:T(1,128)S(1)}, u32[]{:S(2)}, u32[]{:S(2)}) async-start(f32[8,1,1536]{2,1,0:T(1,128)} %reshape.343), calls=%async_computation.3 | async-start | bytes 98304 | tf_op jit(solution)/shard_map/all_to_all | solution.py:116
  140.7 5.3 %all-to-all-done.3 = f32[8,1,1536]{2,1,0:T(1,128)S(1)} async-done(((f32[8,1,1536]{2,1,0:T(1,128)}), f32[8,1,1536]{2,1,0:T(1,128)S(1)}, u32[]{:S(2)}, u32[]{:S(2)}) %all-to-all-start.3) | async-done | bytes 49184 | tf_op jit(solution)/shard_map/all_to_all | solution.py:116
  146.0 0.8 reduce.50
  147.1 0.8 gather_fusion.6
  149.4 1.1 scatter_custom_fusion.4
  150.5 15.7 %psum.15 = f32[5,1024]{0,1:T(8,128)S(1)} all-reduce(f32[5,1024]{0,1:T(8,128)S(1)} %scatter_custom_fusion.4), channel_id=1, replica_groups=mesh['sky'=8,'tm'=4] {'tm'}, use_global_device_ids=true, to_apply=%region_19.23 | all-reduce | flops 5120 | bytes 40960 | tf_op jit(solution)/shard_map/psum | solution.py:132
  166.2 8.5 %fusion.186 = f32[1024,1,5]{2,1,0:T(1,128)S(1)} fusion(f32[5,1024,1]{0,2,1:T(1,128)S(1)} %bitcast.303, f32[5,5,1024]{0,1,2:T(8,128)} %copy.86), kind=kOutput, calls=%fused_computation.313 | convolution fusion | flops 307200 | bytes 143360 | tf_op jit(solution)/shard_map/klm,lm->km/dot_general | solution.py:133
  177.0 4.3 %scatter_fusion.2 = f32[3,16,256]{1,0,2:T(4,128)S(1)} fusion(f32[3,16,256]{1,0,2:T(4,128)S(1)} %broadcast.97, s32[128]{0:T(128)S(1)} %get-tuple-element.44, f32[128,3,16]{2,1,0:T(4,128)S(1)} %copy.81), kind=kCustom, calls=%fused_computation.13 | custom fusion | bytes 74240 | tf_op jit(solution)/shard_map/scatter | solution.py:149
  181.7 8.1 %all_to_all.35 = f32[8,1,1536]{2,1,0:T(1,128)S(1)} all-to-all(f32[8,1,1536]{2,1,0:T(1,128)S(1)} %reshape.345), channel_id=1, replica_groups=mesh['sky'=8,'tm'=4] {'sky'}, dimensions={0} | all-to-all | bytes 98304 | tf_op jit(solution)/shard_map/all_to_all | solution.py:151
  189.8 0.8 reduce.51
  191.0 8.8 %scatter_fusion.3 = f32[3,16,33]{1,0,2:T(4,128)S(1)} fusion(f32[3,16,33]{1,0,2:T(4,128)S(1)} %broadcast.94, s32[256]{0:T(256)S(1)} %bitcast.317, f32[256,3,16]{2,1,0:T(4,128)S(1)} %bitcast_bitcast_fusion), kind=kCustom, calls=%fused_computation.14 | custom fusion | flops 12288 | bytes 148480 | tf_op jit(solution)/shard_map/scatter-add | solution.py:153
  200.2 4.0 %collective-permute-start.10 = (f32[3,16]{1,0:T(4,128)S(1)}, f32[3,16]{1,0:T(4,128)S(1)}, u32[]{:S(2)}, u32[]{:S(2)}) collective-permute-start(f32[3,16]{1,0:T(4,128)S(1)} %get-tuple-element.65), channel_id=1, source_target_pairs={{4,0},{8,4},{12,8},{16,12},{20,16},{24,20},{28,24},{0,28},{5,1},{9... | collective-permute-start | bytes 584 | tf_op jit(solution)/shard_map/ppermute | solution.py:22
  204.2 1.0 collective-permute-done.8
  205.2 5.4 %collective-permute-start.9 = (f32[3,16]{1,0:T(4,128)S(1)}, f32[3,16]{1,0:T(4,128)S(1)}, u32[]{:S(2)}, u32[]{:S(2)}) collective-permute-start(f32[3,16]{1,0:T(4,128)S(1)} %collective-permute-done.8), channel_id=1, source_target_pairs={{0,1},{1,2},{2,3},{4,5},{5,6},{6,7},{8,9},{9,10},{10,11},{12,13},{... | collective-permute-start | bytes 584 | tf_op jit(solution)/shard_map/ppermute | solution.py:30
  210.6 1.9 collective-permute-start.11
  212.5 3.0 %collective-permute-done.11 = f32[3,16]{1,0:T(4,128)S(1)} collective-permute-done((f32[3,16]{1,0:T(4,128)S(1)}, f32[3,16]{1,0:T(4,128)S(1)}, u32[]{:S(2)}, u32[]{:S(2)}) %collective-permute-start.11) | collective-permute-done | bytes 224 | tf_op jit(solution)/shard_map/ppermute | solution.py:30
  215.8 4.2 %collective-permute-start.14 = (f32[3,16]{1,0:T(4,128)S(1)}, f32[3,16]{1,0:T(4,128)S(1)}, u32[]{:S(2)}, u32[]{:S(2)}) collective-permute-start(f32[3,16]{1,0:T(4,128)S(1)} %get-tuple-element.63), channel_id=1, source_target_pairs={{4,0},{8,4},{12,8},{16,12},{20,16},{24,20},{28,24},{0,28},{5,1},{9... | collective-permute-start | bytes 584 | tf_op jit(solution)/shard_map/ppermute | solution.py:22
  220.0 0.9 collective-permute-done.12
  220.9 3.1 %collective-permute-start.13 = (f32[3,16]{1,0:T(4,128)S(1)}, f32[3,16]{1,0:T(4,128)S(1)}, u32[]{:S(2)}, u32[]{:S(2)}) collective-permute-start(f32[3,16]{1,0:T(4,128)S(1)} %collective-permute-done.12), channel_id=1, source_target_pairs={{0,1},{1,2},{2,3},{4,5},{5,6},{6,7},{8,9},{9,10},{10,11},{12,13},{... | collective-permute-start | bytes 584 | tf_op jit(solution)/shard_map/ppermute | solution.py:30
  224.0 0.8 copy.83
  224.8 1.9 collective-permute-start.15
  226.7 3.0 %collective-permute-done.15 = f32[3,16]{1,0:T(4,128)S(1)} collective-permute-done((f32[3,16]{1,0:T(4,128)S(1)}, f32[3,16]{1,0:T(4,128)S(1)}, u32[]{:S(2)}, u32[]{:S(2)}) %collective-permute-start.15) | collective-permute-done | bytes 224 | tf_op jit(solution)/shard_map/ppermute | solution.py:30
  (130 shorter events, 16.6 us)
Async XLA Ops:
  0.6 30.3 %copy-start = (f32[3,3,1,512]{3,2,1,0:T(1,128)S(1)}, f32[3,3,1,512]{3,2,1,0:T(1,128)}, u32[]{:S(2)}) copy-start(f32[3,3,1,512]{3,2,1,0:T(1,128)} %param.27) | copy-start | bytes 55300
  3.4 27.6 %all-to-all-start = ((s32[8,32,1]{1,2,0:T(1,128)}), s32[8,32,1]{1,2,0:T(1,128)S(1)}, u32[]{:S(2)}, u32[]{:S(2)}) async-start(s32[8,32,1]{1,2,0:T(1,128)} %bitcast.8), calls=%async_computation | async-start | bytes 8192 | tf_op jit(solution)/shard_map/all_to_all | solution.py:109
  34.7 11.1 %all-to-all-start.1 = ((f32[8,1,1536]{2,1,0:T(1,128)}), f32[8,1,1536]{2,1,0:T(1,128)S(1)}, u32[]{:S(2)}, u32[]{:S(2)}) async-start(f32[8,1,1536]{2,1,0:T(1,128)} %reshape.339), calls=%async_computation.1 | async-start | bytes 98304 | tf_op jit(solution)/shard_map/all_to_all | solution.py:116
  77.7 27.7 %copy-start.2 = (f32[3,1,512]{2,1,0:T(1,128)S(1)}, f32[3,1,512]{2,1,0:T(1,128)}, u32[]{:S(2)}) copy-start(f32[3,1,512]{2,1,0:T(1,128)} %param.28) | copy-start | bytes 18436
  77.7 56.8 %copy-start.1 = (f32[3,1,512]{2,1,0:T(1,128)S(1)}, f32[3,1,512]{2,1,0:T(1,128)}, u32[]{:S(2)}) copy-start(f32[3,1,512]{2,1,0:T(1,128)} %param.26) | copy-start | bytes 18436
  86.0 9.1 %all-to-all-start.2 = ((f32[8,1,1536]{2,1,0:T(1,128)}), f32[8,1,1536]{2,1,0:T(1,128)S(1)}, u32[]{:S(2)}, u32[]{:S(2)}) async-start(f32[8,1,1536]{2,1,0:T(1,128)} %reshape.341), calls=%async_computation.2 | async-start | bytes 98304 | tf_op jit(solution)/shard_map/all_to_all | solution.py:151
  105.4 5.1 %collective-permute-start = (f32[3,16]{1,0:T(4,128)S(1)}, f32[3,16]{1,0:T(4,128)S(1)}, u32[]{:S(2)}, u32[]{:S(2)}) collective-permute-start(f32[3,16]{1,0:T(4,128)S(1)} %get-tuple-element.68), channel_id=1, source_target_pairs={{0,4},{4,8},{8,12},{12,16},{16,20},{20,24},{24,28},{28,0},{1,5},{5... | collective-permute-start | bytes 584 | tf_op jit(solution)/shard_map/ppermute | solution.py:19
  105.7 10.4 %collective-permute-start.2 = (f32[3,16]{1,0:T(4,128)S(1)}, f32[3,16]{1,0:T(4,128)S(1)}, u32[]{:S(2)}, u32[]{:S(2)}) collective-permute-start(f32[3,16]{1,0:T(4,128)S(1)} %get-tuple-element.69), channel_id=1, source_target_pairs={{4,0},{8,4},{12,8},{16,12},{20,16},{24,20},{28,24},{0,28},{5,1},{9... | collective-permute-start | bytes 584 | tf_op jit(solution)/shard_map/ppermute | solution.py:22
  110.6 7.5 %collective-permute-start.1 = (f32[3,16]{1,0:T(4,128)S(1)}, f32[3,16]{1,0:T(4,128)S(1)}, u32[]{:S(2)}, u32[]{:S(2)}) collective-permute-start(f32[3,16]{1,0:T(4,128)S(1)} %collective-permute-done), channel_id=1, source_target_pairs={{0,1},{1,2},{2,3},{4,5},{5,6},{6,7},{8,9},{9,10},{10,11},{12,13},{... | collective-permute-start | bytes 584 | tf_op jit(solution)/shard_map/ppermute | solution.py:30
  116.1 4.9 %collective-permute-start.3 = (f32[3,16]{1,0:T(4,128)S(1)}, f32[3,16]{1,0:T(4,128)S(1)}, u32[]{:S(2)}, u32[]{:S(2)}) collective-permute-start(f32[3,16]{1,0:T(4,128)S(1)} %collective-permute-done.2), channel_id=1, source_target_pairs={{1,0},{2,1},{3,2},{5,4},{6,5},{7,6},{9,8},{10,9},{11,10},{13,12},{... | collective-permute-start | bytes 584 | tf_op jit(solution)/shard_map/ppermute | solution.py:30
  121.3 5.1 %collective-permute-start.4 = (f32[3,16]{1,0:T(4,128)S(1)}, f32[3,16]{1,0:T(4,128)S(1)}, u32[]{:S(2)}, u32[]{:S(2)}) collective-permute-start(f32[3,16]{1,0:T(4,128)S(1)} %get-tuple-element.66), channel_id=1, source_target_pairs={{0,4},{4,8},{8,12},{12,16},{16,20},{20,24},{24,28},{28,0},{1,5},{5... | collective-permute-start | bytes 584 | tf_op jit(solution)/shard_map/ppermute | solution.py:19
  121.3 8.2 %collective-permute-start.6 = (f32[3,16]{1,0:T(4,128)S(1)}, f32[3,16]{1,0:T(4,128)S(1)}, u32[]{:S(2)}, u32[]{:S(2)}) collective-permute-start(f32[3,16]{1,0:T(4,128)S(1)} %get-tuple-element.67), channel_id=1, source_target_pairs={{4,0},{8,4},{12,8},{16,12},{20,16},{24,20},{28,24},{0,28},{5,1},{9... | collective-permute-start | bytes 584 | tf_op jit(solution)/shard_map/ppermute | solution.py:22
  126.4 5.0 %collective-permute-start.5 = (f32[3,16]{1,0:T(4,128)S(1)}, f32[3,16]{1,0:T(4,128)S(1)}, u32[]{:S(2)}, u32[]{:S(2)}) collective-permute-start(f32[3,16]{1,0:T(4,128)S(1)} %collective-permute-done.4), channel_id=1, source_target_pairs={{0,1},{1,2},{2,3},{4,5},{5,6},{6,7},{8,9},{9,10},{10,11},{12,13},{... | collective-permute-start | bytes 584 | tf_op jit(solution)/shard_map/ppermute | solution.py:30
  129.5 4.9 %collective-permute-start.7 = (f32[3,16]{1,0:T(4,128)S(1)}, f32[3,16]{1,0:T(4,128)S(1)}, u32[]{:S(2)}, u32[]{:S(2)}) collective-permute-start(f32[3,16]{1,0:T(4,128)S(1)} %collective-permute-done.6), channel_id=1, source_target_pairs={{1,0},{2,1},{3,2},{5,4},{6,5},{7,6},{9,8},{10,9},{11,10},{13,12},{... | collective-permute-start | bytes 584 | tf_op jit(solution)/shard_map/ppermute | solution.py:30
  137.1 8.9 %all-to-all-start.3 = ((f32[8,1,1536]{2,1,0:T(1,128)}), f32[8,1,1536]{2,1,0:T(1,128)S(1)}, u32[]{:S(2)}, u32[]{:S(2)}) async-start(f32[8,1,1536]{2,1,0:T(1,128)} %reshape.343), calls=%async_computation.3 | async-start | bytes 98304 | tf_op jit(solution)/shard_map/all_to_all | solution.py:116
  200.0 5.1 %collective-permute-start.8 = (f32[3,16]{1,0:T(4,128)S(1)}, f32[3,16]{1,0:T(4,128)S(1)}, u32[]{:S(2)}, u32[]{:S(2)}) collective-permute-start(f32[3,16]{1,0:T(4,128)S(1)} %get-tuple-element.64), channel_id=1, source_target_pairs={{0,4},{4,8},{8,12},{12,16},{16,20},{20,24},{24,28},{28,0},{1,5},{5... | collective-permute-start | bytes 584 | tf_op jit(solution)/shard_map/ppermute | solution.py:19
  200.2 10.4 %collective-permute-start.10 = (f32[3,16]{1,0:T(4,128)S(1)}, f32[3,16]{1,0:T(4,128)S(1)}, u32[]{:S(2)}, u32[]{:S(2)}) collective-permute-start(f32[3,16]{1,0:T(4,128)S(1)} %get-tuple-element.65), channel_id=1, source_target_pairs={{4,0},{8,4},{12,8},{16,12},{20,16},{24,20},{28,24},{0,28},{5,1},{9... | collective-permute-start | bytes 584 | tf_op jit(solution)/shard_map/ppermute | solution.py:22
  205.2 7.3 %collective-permute-start.9 = (f32[3,16]{1,0:T(4,128)S(1)}, f32[3,16]{1,0:T(4,128)S(1)}, u32[]{:S(2)}, u32[]{:S(2)}) collective-permute-start(f32[3,16]{1,0:T(4,128)S(1)} %collective-permute-done.8), channel_id=1, source_target_pairs={{0,1},{1,2},{2,3},{4,5},{5,6},{6,7},{8,9},{9,10},{10,11},{12,13},{... | collective-permute-start | bytes 584 | tf_op jit(solution)/shard_map/ppermute | solution.py:30
  210.6 4.9 %collective-permute-start.11 = (f32[3,16]{1,0:T(4,128)S(1)}, f32[3,16]{1,0:T(4,128)S(1)}, u32[]{:S(2)}, u32[]{:S(2)}) collective-permute-start(f32[3,16]{1,0:T(4,128)S(1)} %collective-permute-done.10), channel_id=1, source_target_pairs={{1,0},{2,1},{3,2},{5,4},{6,5},{7,6},{9,8},{10,9},{11,10},{13,12},{... | collective-permute-start | bytes 584 | tf_op jit(solution)/shard_map/ppermute | solution.py:30
  215.7 5.1 %collective-permute-start.12 = (f32[3,16]{1,0:T(4,128)S(1)}, f32[3,16]{1,0:T(4,128)S(1)}, u32[]{:S(2)}, u32[]{:S(2)}) collective-permute-start(f32[3,16]{1,0:T(4,128)S(1)} %get-tuple-element.62), channel_id=1, source_target_pairs={{0,4},{4,8},{8,12},{12,16},{16,20},{20,24},{24,28},{28,0},{1,5},{5... | collective-permute-start | bytes 584 | tf_op jit(solution)/shard_map/ppermute | solution.py:19
  215.8 9.0 %collective-permute-start.14 = (f32[3,16]{1,0:T(4,128)S(1)}, f32[3,16]{1,0:T(4,128)S(1)}, u32[]{:S(2)}, u32[]{:S(2)}) collective-permute-start(f32[3,16]{1,0:T(4,128)S(1)} %get-tuple-element.63), channel_id=1, source_target_pairs={{4,0},{8,4},{12,8},{16,12},{20,16},{24,20},{28,24},{0,28},{5,1},{9... | collective-permute-start | bytes 584 | tf_op jit(solution)/shard_map/ppermute | solution.py:22
  220.9 5.8 %collective-permute-start.13 = (f32[3,16]{1,0:T(4,128)S(1)}, f32[3,16]{1,0:T(4,128)S(1)}, u32[]{:S(2)}, u32[]{:S(2)}) collective-permute-start(f32[3,16]{1,0:T(4,128)S(1)} %collective-permute-done.12), channel_id=1, source_target_pairs={{0,1},{1,2},{2,3},{4,5},{5,6},{6,7},{8,9},{9,10},{10,11},{12,13},{... | collective-permute-start | bytes 584 | tf_op jit(solution)/shard_map/ppermute | solution.py:30
  224.8 4.9 %collective-permute-start.15 = (f32[3,16]{1,0:T(4,128)S(1)}, f32[3,16]{1,0:T(4,128)S(1)}, u32[]{:S(2)}, u32[]{:S(2)}) collective-permute-start(f32[3,16]{1,0:T(4,128)S(1)} %collective-permute-done.14), channel_id=1, source_target_pairs={{1,0},{2,1},{3,2},{5,4},{6,5},{7,6},{9,8},{10,9},{11,10},{13,12},{... | collective-permute-start | bytes 584 | tf_op jit(solution)/shard_map/ppermute | solution.py:30
where the time goes:
time: 232 us; the launch traced here: 230 us
  starting transfers between devices  60.1 us (26%)
  blocking collectives  42.1 us (18%)
  local copies, waits for them, and re-layouts  37 us (16%)
  waiting for transfers between devices  32.1 us (14%)
  other arithmetic  28.5 us (12%)
  matrix products  20.9 us (9%)
  between operations  9.85 us (4%)
    psum x2, blocking collectives, per_device(): normal = lax.psum(local_normal, 'tm')  34 us
    ppermute x8, starting transfers between devices, from_behind(): lax.ppermute(value, axis, [(source, source + steps) for source in range(i...  24.7 us
    scatter-add x2, other arithmetic, per_device(): jnp.zeros((3, BLOCK_KNOTS, blocks_here + 1), jnp.float32).at[:, :, wanted]  17.6 us
    dot_general x2, matrix products, per_device(): jnp.einsum('klm,lm->km', inverses, normal, precision=lax.Precision.HIGHEST)  17.1 us
    ppermute x4, starting transfers between devices, padded_2(): lax.ppermute(lax.slice_in_dim(block, 0, width, axis=dim), axis, backward)  16.3 us
    unnamed x27, local copies, waits for them, and re-layouts  12.5 us
    ppermute x8, waiting for transfers between devices, from_behind(): lax.ppermute(value, axis, [(source, source + steps) for source in range(i...  11.8 us
    all_to_all x2, waiting for transfers between devices, per_device(): lax.all_to_all(served, 'sky', split_axis=2, concat_axis=2, tiled=True)  10.9 us
  transfers between devices with their start and end apart: 20, of which 11 were waited for; matrix products, arithmetic and copies ran while one was open for 6% of the time, Pallas kernels for 0%

commit v1 on v0

--- a/solution.py
+++ b/solution.py
@@ -113,7 +113,19 @@
             [knots_now.reshape(3, blocks_here, BLOCK_KNOTS), spare], axis=1
         )
         served = jnp.take(jnp.transpose(own_blocks, (0, 2, 1)), wanted, axis=2)
-        arrived = lax.all_to_all(served, "sky", split_axis=2, concat_axis=2, tiled=True)
+        ways, here = (lax.axis_size("sky"), lax.axis_index("sky"))
+        width_2 = served.shape[2] // ways
+        dims = list(served.shape)
+        dims[2] = width_2
+        height = dims[2]
+        dims[2] = height * ways
+        full = jnp.zeros(dims, served.dtype)
+        for mask in range(ways):
+            part = lax.dynamic_slice_in_dim(served, (here ^ mask) * width_2, width_2, axis=2)
+            if mask:
+                part = lax.ppermute(part, "sky", [(d, d ^ mask) for d in range(ways)])
+            full = lax.dynamic_update_slice_in_dim(full, part, (here ^ mask) * height, axis=2)
+        arrived = full
         fetched = jnp.transpose(jnp.take(arrived, column, axis=2), (0, 2, 1))
         att_term = jnp.zeros(observed.shape, jnp.float32)
         for axis_index in range(3):

time: 232 us -> 240 us (1.034)
  starting transfers between devices: 60.1 us -> 70.1 us
  blocking collectives: 42.1 us -> 46.5 us
  local copies, waits for them, and re-layouts: 37 us -> 33.3 us
    ppermute x0 -> x14, starting transfers between devices: none -> 18.8 us  [per_device(): part = lax.ppermute(part, 'sky', [(d, d ^ mask) for d in range(ways)])]
    all_to_all x2 -> x0, waiting for transfers between devices: 10.9 us -> none  [per_device(): lax.all_to_all(served, 'sky', split_axis=2, concat_axis=2, tiled=True)]
    ppermute x0 -> x14, waiting for transfers between devices: none -> 10.2 us  [per_device(): part = lax.ppermute(part, 'sky', [(d, d ^ mask) for d in range(ways)])]
    all_to_all x2 -> x0, starting transfers between devices: 8.78 us -> none  [per_device(): lax.all_to_all(served, 'sky', split_axis=2, concat_axis=2, tiled=True)]
    unnamed x27, local copies, waits for them, and re-layouts: 12.5 us -> 8.17 us
    all_to_all x1, blocking collectives: 8.06 us -> 10.9 us  [per_device(): lax.all_to_all(outgoing, 'sky', split_axis=2, concat_axis=2, tiled=True)]
  transfers between devices with their start and end apart: 20 -> 32, of which waited for: 11 -> 12; matrix products, arithmetic and copies ran while one was open for 6% -> 5% of each run, Pallas kernels for 0% -> 0%
where the time goes in v1:
time: 240 us; the launch traced here: 239 us
  starting transfers between devices  70.1 us (29%)
  blocking collectives  46.5 us (19%)
  local copies, waits for them, and re-layouts  33.3 us (14%)
  waiting for transfers between devices  31.4 us (13%)
  other arithmetic  27 us (11%)
  matrix products  20.9 us (9%)
  between operations  9.71 us (4%)
    psum x2, blocking collectives, per_device(): normal = lax.psum(local_normal, 'tm')  35.6 us
    ppermute x8, starting transfers between devices, from_behind(): lax.ppermute(value, axis, [(source, source + steps) for source in range(i...  24.9 us
    ppermute x14, starting transfers between devices, per_device(): part = lax.ppermute(part, 'sky', [(d, d ^ mask) for d in range(ways)])  18.8 us
    scatter-add x2, other arithmetic, per_device(): jnp.zeros((3, BLOCK_KNOTS, blocks_here + 1), jnp.float32).at[:, :, wanted]  17.6 us
    dot_general x2, matrix products, per_device(): jnp.einsum('klm,lm->km', inverses, normal, precision=lax.Precision.HIGHEST)  17.1 us
    ppermute x4, starting transfers between devices, padded_2(): lax.ppermute(lax.slice_in_dim(block, 0, width, axis=dim), axis, backward)  16.6 us
    ppermute x8, waiting for transfers between devices, from_behind(): lax.ppermute(value, axis, [(source, source + steps) for source in range(i...  11.8 us
    all_to_all x1, blocking collectives, per_device(): lax.all_to_all(outgoing, 'sky', split_axis=2, concat_axis=2, tiled=True)  10.9 us
  transfers between devices with their start and end apart: 32, of which 12 were waited for; matrix products, arithmetic and copies ran while one was open for 5% of the time, Pallas kernels for 0%

profile of v1, /device:TPU:1, one launch (start us, length us, event | category | flops | bytes accessed | tf_op | source)
XLA Modules:
  0.0 238.9 jit_solution(16156491564012795584)
XLA Ops:
  0.6 0.7 and_select_fusion
  1.8 1.0 scatter_custom_fusion
  2.8 0.7 all_to_all.16
  3.5 6.3 %all-to-all-start = ((s32[8,32,1]{1,2,0:T(1,128)}), s32[8,32,1]{1,2,0:T(1,128)S(1)}, u32[]{:S(2)}, u32[]{:S(2)}) async-start(s32[8,32,1]{1,2,0:T(1,128)} %bitcast.8), calls=%async_computation | async-start | bytes 8192 | tf_op jit(solution)/shard_map/all_to_all | solution.py:109
  10.5 0.7 reduce.7
  11.4 0.8 fusion.188
  12.2 1.0 copy.72
  14.2 0.8 fusion.187
  15.1 1.4 fusion.194
  16.4 0.7 fusion.189
  19.1 1.0 gather_fusion.1
  20.7 1.5 collective-permute-start
  30.6 2.7 %copy.86 = f32[5,5,1024]{0,1,2:T(8,128)} copy(f32[5,5,1024]{2,1,0:T(8,128)S(1)} %copy-done) | data formatting | bytes 204800 | tf_op args[7]
  33.5 1.2 collective-permute-start.1
  34.8 2.3 collective-permute-start.3
  37.1 1.2 collective-permute-start.4
  38.3 3.0 %collective-permute-start.5 = (f32[3,16,32]{1,0,2:T(4,128)S(1)}, f32[3,16,32]{1,0,2:T(4,128)S(1)}, u32[]{:S(2)}, u32[]{:S(2)}) collective-permute-start(f32[3,16,32]{1,0,2:T(4,128)S(1)} %get-tuple-element.54), channel_id=1, source_target_pairs={{0,24},{4,28},{8,16},{12,20},{16,8},{20,12},{24,0},{28,4},{1,25},{... | collective-permute-start | bytes 18440 | tf_op jit(solution)/shard_map/ppermute | solution.py:126
  41.6 5.9 %collective-permute-done.4 = f32[3,16,32]{1,0,2:T(4,128)S(1)} collective-permute-done((f32[3,16,32]{1,0,2:T(4,128)S(1)}, f32[3,16,32]{1,0,2:T(4,128)S(1)}, u32[]{:S(2)}, u32[]{:S(2)}) %collective-permute-start.4) | collective-permute-done | bytes 6176 | tf_op jit(solution)/shard_map/ppermute | solution.py:126
  47.5 0.8 gather_fusion.2
  49.8 1.1 scatter_custom_fusion.1
  50.9 19.8 %psum.14 = f32[5,1024]{0,1:T(8,128)S(1)} all-reduce(f32[5,1024]{0,1:T(8,128)S(1)} %scatter_custom_fusion.1), channel_id=1, replica_groups=mesh['sky'=8,'tm'=4] {'tm'}, use_global_device_ids=true, to_apply=%region_9.13 | all-reduce | flops 5120 | bytes 40960 | tf_op jit(solution)/shard_map/psum | solution.py:144
  70.7 8.5 %fusion.195 = f32[1024,1,5]{2,1,0:T(1,128)S(1)} fusion(f32[5,1024,1]{0,2,1:T(1,128)S(1)} %bitcast.246, f32[5,5,1024]{0,1,2:T(8,128)} %copy.86), kind=kOutput, calls=%fused_computation.376 | convolution fusion | flops 307200 | bytes 143360 | tf_op jit(solution)/shard_map/klm,lm->km/dot_general | solution.py:145
  82.3 4.3 %scatter_fusion = f32[3,16,256]{1,0,2:T(4,128)S(1)} fusion(f32[3,16,256]{1,0,2:T(4,128)S(1)} %broadcast.93.clone.1, s32[128]{0:T(128)S(1)} %get-tuple-element.44, f32[128,3,16]{2,1,0:T(4,128)S(1)} %copy.74), kind=kCustom, calls=%fused_computation.10 | custom fusion | bytes 74240 | tf_op jit(solution)/shard_map/scatter | solution.py:161
  86.6 1.0 reshape.339
  87.6 3.3 %all-to-all-start.1 = ((f32[8,1,1536]{2,1,0:T(1,128)}), f32[8,1,1536]{2,1,0:T(1,128)S(1)}, u32[]{:S(2)}, u32[]{:S(2)}) async-start(f32[8,1,1536]{2,1,0:T(1,128)} %reshape.339), calls=%async_computation.1 | async-start | bytes 98304 | tf_op jit(solution)/shard_map/all_to_all | solution.py:163
  90.9 5.6 %all-to-all-done.1 = f32[8,1,1536]{2,1,0:T(1,128)S(1)} async-done(((f32[8,1,1536]{2,1,0:T(1,128)}), f32[8,1,1536]{2,1,0:T(1,128)S(1)}, u32[]{:S(2)}, u32[]{:S(2)}) %all-to-all-start.1) | async-done | bytes 49184 | tf_op jit(solution)/shard_map/all_to_all | solution.py:163
  97.0 0.8 reduce.48
  98.2 8.8 %scatter_fusion.1 = f32[3,16,33]{1,0,2:T(4,128)S(1)} fusion(f32[3,16,33]{1,0,2:T(4,128)S(1)} %broadcast.98.clone, s32[256]{0:T(256)S(1)} %bitcast.256, f32[256,3,16]{2,1,0:T(4,128)S(1)} %bitcast_bitcast_fusion.1), kind=kCustom, calls=%fused_computation.11 | custom fusion | flops 12288 | bytes 148480 | tf_op jit(solution)/shard_map/scatter-add | solution.py:165
  107.4 4.1 %collective-permute-start.9 = (f32[3,16]{1,0:T(4,128)S(1)}, f32[3,16]{1,0:T(4,128)S(1)}, u32[]{:S(2)}, u32[]{:S(2)}) collective-permute-start(f32[3,16]{1,0:T(4,128)S(1)} %get-tuple-element.85), channel_id=1, source_target_pairs={{4,0},{8,4},{12,8},{16,12},{20,16},{24,20},{28,24},{0,28},{5,1},{9... | collective-permute-start | bytes 584 | tf_op jit(solution)/shard_map/ppermute | solution.py:22
  111.4 1.0 collective-permute-done.7
  112.4 5.6 %collective-permute-start.8 = (f32[3,16]{1,0:T(4,128)S(1)}, f32[3,16]{1,0:T(4,128)S(1)}, u32[]{:S(2)}, u32[]{:S(2)}) collective-permute-start(f32[3,16]{1,0:T(4,128)S(1)} %collective-permute-done.7), channel_id=1, source_target_pairs={{0,1},{1,2},{2,3},{4,5},{5,6},{6,7},{8,9},{9,10},{10,11},{12,13},{... | collective-permute-start | bytes 584 | tf_op jit(solution)/shard_map/ppermute | solution.py:30
  118.1 1.9 collective-permute-start.10
  120.0 3.0 %collective-permute-done.10 = f32[3,16]{1,0:T(4,128)S(1)} collective-permute-done((f32[3,16]{1,0:T(4,128)S(1)}, f32[3,16]{1,0:T(4,128)S(1)}, u32[]{:S(2)}, u32[]{:S(2)}) %collective-permute-start.10) | collective-permute-done | bytes 224 | tf_op jit(solution)/shard_map/ppermute | solution.py:30
  123.2 4.2 %collective-permute-start.13 = (f32[3,16]{1,0:T(4,128)S(1)}, f32[3,16]{1,0:T(4,128)S(1)}, u32[]{:S(2)}, u32[]{:S(2)}) collective-permute-start(f32[3,16]{1,0:T(4,128)S(1)} %get-tuple-element.83), channel_id=1, source_target_pairs={{4,0},{8,4},{12,8},{16,12},{20,16},{24,20},{28,24},{0,28},{5,1},{9... | collective-permute-start | bytes 584 | tf_op jit(solution)/shard_map/ppermute | solution.py:22
  127.4 1.0 collective-permute-done.11
  128.4 3.1 %collective-permute-start.12 = (f32[3,16]{1,0:T(4,128)S(1)}, f32[3,16]{1,0:T(4,128)S(1)}, u32[]{:S(2)}, u32[]{:S(2)}) collective-permute-start(f32[3,16]{1,0:T(4,128)S(1)} %collective-permute-done.11), channel_id=1, source_target_pairs={{0,1},{1,2},{2,3},{4,5},{5,6},{6,7},{8,9},{9,10},{10,11},{12,13},{... | collective-permute-start | bytes 584 | tf_op jit(solution)/shard_map/ppermute | solution.py:30
  131.5 1.9 collective-permute-start.14
  133.4 3.0 %collective-permute-done.14 = f32[3,16]{1,0:T(4,128)S(1)} collective-permute-done((f32[3,16]{1,0:T(4,128)S(1)}, f32[3,16]{1,0:T(4,128)S(1)}, u32[]{:S(2)}, u32[]{:S(2)}) %collective-permute-start.14) | collective-permute-done | bytes 224 | tf_op jit(solution)/shard_map/ppermute | solution.py:30
  136.7 1.0 gather_fusion.5
  138.7 2.6 %collective-permute-start.17 = (f32[3,16,32]{1,0,2:T(4,128)S(1)}, f32[3,16,32]{1,0,2:T(4,128)S(1)}, u32[]{:S(2)}, u32[]{:S(2)}) collective-permute-start(f32[3,16,32]{1,0,2:T(4,128)S(1)} %get-tuple-element.49), channel_id=1, source_target_pairs={{0,12},{4,8},{8,4},{12,0},{16,28},{20,24},{24,20},{28,16},{1,13},{... | collective-permute-start | bytes 18440 | tf_op jit(solution)/shard_map/ppermute | solution.py:126
  141.3 2.1 collective-permute-start.19
  143.4 1.3 collective-permute-start.20
  144.8 3.2 %collective-permute-start.21 = (f32[3,16,32]{1,0,2:T(4,128)S(1)}, f32[3,16,32]{1,0,2:T(4,128)S(1)}, u32[]{:S(2)}, u32[]{:S(2)}) collective-permute-start(f32[3,16,32]{1,0,2:T(4,128)S(1)} %get-tuple-element.45), channel_id=1, source_target_pairs={{0,28},{4,24},{8,20},{12,16},{16,12},{20,8},{24,4},{28,0},{1,29},{... | collective-permute-start | bytes 18440 | tf_op jit(solution)/shard_map/ppermute | solution.py:126
  148.0 3.0 %collective-permute-done.18 = f32[3,16,32]{1,0,2:T(4,128)S(1)} collective-permute-done((f32[3,16,32]{1,0,2:T(4,128)S(1)}, f32[3,16,32]{1,0,2:T(4,128)S(1)}, u32[]{:S(2)}, u32[]{:S(2)}) %collective-permute-start.18) | collective-permute-done | bytes 6176 | tf_op jit(solution)/shard_map/ppermute | solution.py:126
  151.1 1.3 collective-permute-done.19
  152.5 0.8 gather_fusion.6
  154.7 1.1 scatter_custom_fusion.4
  155.8 15.8 %psum.15 = f32[5,1024]{0,1:T(8,128)S(1)} all-reduce(f32[5,1024]{0,1:T(8,128)S(1)} %scatter_custom_fusion.4), channel_id=1, replica_groups=mesh['sky'=8,'tm'=4] {'tm'}, use_global_device_ids=true, to_apply=%region_19.23 | all-reduce | flops 5120 | bytes 40960 | tf_op jit(solution)/shard_map/psum | solution.py:144
  171.6 8.5 %fusion.196 = f32[1024,1,5]{2,1,0:T(1,128)S(1)} fusion(f32[5,1024,1]{0,2,1:T(1,128)S(1)} %bitcast.245, f32[5,5,1024]{0,1,2:T(8,128)} %copy.86), kind=kOutput, calls=%fused_computation.377 | convolution fusion | flops 307200 | bytes 143360 | tf_op jit(solution)/shard_map/klm,lm->km/dot_general | solution.py:145
  182.5 4.3 %scatter_fusion.2 = f32[3,16,256]{1,0,2:T(4,128)S(1)} fusion(f32[3,16,256]{1,0,2:T(4,128)S(1)} %broadcast.93, s32[128]{0:T(128)S(1)} %get-tuple-element.44, f32[128,3,16]{2,1,0:T(4,128)S(1)} %copy.81), kind=kCustom, calls=%fused_computation.13 | custom fusion | bytes 74240 | tf_op jit(solution)/shard_map/scatter | solution.py:161
  187.2 10.9 %all_to_all.25 = f32[8,1,1536]{2,1,0:T(1,128)S(1)} all-to-all(f32[8,1,1536]{2,1,0:T(1,128)S(1)} %reshape.341), channel_id=1, replica_groups=mesh['sky'=8,'tm'=4] {'sky'}, dimensions={0} | all-to-all | bytes 98304 | tf_op jit(solution)/shard_map/all_to_all | solution.py:163
  198.1 0.8 reduce.49
  199.4 8.8 %scatter_fusion.3 = f32[3,16,33]{1,0,2:T(4,128)S(1)} fusion(f32[3,16,33]{1,0,2:T(4,128)S(1)} %broadcast.98, s32[256]{0:T(256)S(1)} %bitcast.257, f32[256,3,16]{2,1,0:T(4,128)S(1)} %bitcast_bitcast_fusion), kind=kCustom, calls=%fused_computation.14 | custom fusion | flops 12288 | bytes 148480 | tf_op jit(solution)/shard_map/scatter-add | solution.py:165
  208.4 4.2 %collective-permute-start.24 = (f32[3,16]{1,0:T(4,128)S(1)}, f32[3,16]{1,0:T(4,128)S(1)}, u32[]{:S(2)}, u32[]{:S(2)}) collective-permute-start(f32[3,16]{1,0:T(4,128)S(1)} %get-tuple-element.81), channel_id=1, source_target_pairs={{4,0},{8,4},{12,8},{16,12},{20,16},{24,20},{28,24},{0,28},{5,1},{9... | collective-permute-start | bytes 584 | tf_op jit(solution)/shard_map/ppermute | solution.py:22
  212.6 1.0 collective-permute-done.22
  213.5 5.5 %collective-permute-start.23 = (f32[3,16]{1,0:T(4,128)S(1)}, f32[3,16]{1,0:T(4,128)S(1)}, u32[]{:S(2)}, u32[]{:S(2)}) collective-permute-start(f32[3,16]{1,0:T(4,128)S(1)} %collective-permute-done.22), channel_id=1, source_target_pairs={{0,1},{1,2},{2,3},{4,5},{5,6},{6,7},{8,9},{9,10},{10,11},{12,13},{... | collective-permute-start | bytes 584 | tf_op jit(solution)/shard_map/ppermute | solution.py:30
  219.0 1.9 collective-permute-start.25
  221.0 3.0 %collective-permute-done.25 = f32[3,16]{1,0:T(4,128)S(1)} collective-permute-done((f32[3,16]{1,0:T(4,128)S(1)}, f32[3,16]{1,0:T(4,128)S(1)}, u32[]{:S(2)}, u32[]{:S(2)}) %collective-permute-start.25) | collective-permute-done | bytes 224 | tf_op jit(solution)/shard_map/ppermute | solution.py:30
  224.2 4.2 %collective-permute-start.28 = (f32[3,16]{1,0:T(4,128)S(1)}, f32[3,16]{1,0:T(4,128)S(1)}, u32[]{:S(2)}, u32[]{:S(2)}) collective-permute-start(f32[3,16]{1,0:T(4,128)S(1)} %get-tuple-element.79), channel_id=1, source_target_pairs={{4,0},{8,4},{12,8},{16,12},{20,16},{24,20},{28,24},{0,28},{5,1},{9... | collective-permute-start | bytes 584 | tf_op jit(solution)/shard_map/ppermute | solution.py:22
  228.5 0.9 collective-permute-done.26
  229.3 3.1 %collective-permute-start.27 = (f32[3,16]{1,0:T(4,128)S(1)}, f32[3,16]{1,0:T(4,128)S(1)}, u32[]{:S(2)}, u32[]{:S(2)}) collective-permute-start(f32[3,16]{1,0:T(4,128)S(1)} %collective-permute-done.26), channel_id=1, source_target_pairs={{0,1},{1,2},{2,3},{4,5},{5,6},{6,7},{8,9},{9,10},{10,11},{12,13},{... | collective-permute-start | bytes 584 | tf_op jit(solution)/shard_map/ppermute | solution.py:30
  232.4 0.8 copy.83
  233.2 1.9 collective-permute-start.29
  235.2 3.0 %collective-permute-done.29 = f32[3,16]{1,0:T(4,128)S(1)} collective-permute-done((f32[3,16]{1,0:T(4,128)S(1)}, f32[3,16]{1,0:T(4,128)S(1)}, u32[]{:S(2)}, u32[]{:S(2)}) %collective-permute-start.29) | collective-permute-done | bytes 224 | tf_op jit(solution)/shard_map/ppermute | solution.py:30
  (170 shorter events, 18.7 us)
Async XLA Ops:
  0.6 29.9 %copy-start.2 = (f32[128,128]{1,0:T(8,128)S(1)}, f32[128,128]{1,0:T(8,128)}, u32[]{:S(2)}) copy-start(f32[128,128]{1,0:T(8,128)} %param.18) | copy-start | bytes 196612
  0.6 30.0 %copy-start = (f32[5,5,1024]{2,1,0:T(8,128)S(1)}, f32[5,5,1024]{2,1,0:T(8,128)}, u32[]{:S(2)}) copy-start(f32[5,5,1024]{2,1,0:T(8,128)} %param.25) | copy-start | bytes 307204
  3.5 14.4 %all-to-all-start = ((s32[8,32,1]{1,2,0:T(1,128)}), s32[8,32,1]{1,2,0:T(1,128)S(1)}, u32[]{:S(2)}, u32[]{:S(2)}) async-start(s32[8,32,1]{1,2,0:T(1,128)} %bitcast.8), calls=%async_computation | async-start | bytes 8192 | tf_op jit(solution)/shard_map/all_to_all | solution.py:109
  14.2 19.2 %copy-start.1 = (f32[3,3,1,512]{3,2,1,0:T(1,128)S(1)}, f32[3,3,1,512]{3,2,1,0:T(1,128)}, u32[]{:S(2)}) copy-start(f32[3,3,1,512]{3,2,1,0:T(1,128)} %param.27) | copy-start | bytes 55300
  20.7 17.6 %collective-permute-start = (f32[3,16,32]{1,0,2:T(4,128)S(1)}, f32[3,16,32]{1,0,2:T(4,128)S(1)}, u32[]{:S(2)}, u32[]{:S(2)}) collective-permute-start(f32[3,16,32]{1,0,2:T(4,128)S(1)} %get-tuple-element.59), channel_id=1, source_target_pairs={{0,4},{4,0},{8,12},{12,8},{16,20},{20,16},{24,28},{28,24},{1,5},{5... | collective-permute-start | bytes 18440 | tf_op jit(solution)/shard_map/ppermute | solution.py:126
  33.5 7.9 %collective-permute-start.1 = (f32[3,16,32]{1,0,2:T(4,128)S(1)}, f32[3,16,32]{1,0,2:T(4,128)S(1)}, u32[]{:S(2)}, u32[]{:S(2)}) collective-permute-start(f32[3,16,32]{1,0,2:T(4,128)S(1)} %get-tuple-element.58), channel_id=1, source_target_pairs={{0,8},{4,12},{8,0},{12,4},{16,24},{20,28},{24,16},{28,20},{1,9},{5... | collective-permute-start | bytes 18440 | tf_op jit(solution)/shard_map/ppermute | solution.py:126
  34.7 6.8 %collective-permute-start.2 = (f32[3,16,32]{1,0,2:T(4,128)S(1)}, f32[3,16,32]{1,0,2:T(4,128)S(1)}, u32[]{:S(2)}, u32[]{:S(2)}) collective-permute-start(f32[3,16,32]{1,0,2:T(4,128)S(1)} %get-tuple-element.57), channel_id=1, source_target_pairs={{0,12},{4,8},{8,4},{12,0},{16,28},{20,24},{24,20},{28,16},{1,13},{... | collective-permute-start | bytes 18440 | tf_op jit(solution)/shard_map/ppermute | solution.py:126
  34.8 6.8 %collective-permute-start.3 = (f32[3,16,32]{1,0,2:T(4,128)S(1)}, f32[3,16,32]{1,0,2:T(4,128)S(1)}, u32[]{:S(2)}, u32[]{:S(2)}) collective-permute-start(f32[3,16,32]{1,0,2:T(4,128)S(1)} %get-tuple-element.56), channel_id=1, source_target_pairs={{0,16},{4,20},{8,24},{12,28},{16,0},{20,4},{24,8},{28,12},{1,17},{... | collective-permute-start | bytes 18440 | tf_op jit(solution)/shard_map/ppermute | solution.py:126
  37.1 10.4 %collective-permute-start.4 = (f32[3,16,32]{1,0,2:T(4,128)S(1)}, f32[3,16,32]{1,0,2:T(4,128)S(1)}, u32[]{:S(2)}, u32[]{:S(2)}) collective-permute-start(f32[3,16,32]{1,0,2:T(4,128)S(1)} %get-tuple-element.55), channel_id=1, source_target_pairs={{0,20},{4,16},{8,28},{12,24},{16,4},{20,0},{24,12},{28,8},{1,21},{... | collective-permute-start | bytes 18440 | tf_op jit(solution)/shard_map/ppermute | solution.py:126
  38.3 9.1 %collective-permute-start.5 = (f32[3,16,32]{1,0,2:T(4,128)S(1)}, f32[3,16,32]{1,0,2:T(4,128)S(1)}, u32[]{:S(2)}, u32[]{:S(2)}) collective-permute-start(f32[3,16,32]{1,0,2:T(4,128)S(1)} %get-tuple-element.54), channel_id=1, source_target_pairs={{0,24},{4,28},{8,16},{12,20},{16,8},{20,12},{24,0},{28,4},{1,25},{... | collective-permute-start | bytes 18440 | tf_op jit(solution)/shard_map/ppermute | solution.py:126
  41.3 6.2 %collective-permute-start.6 = (f32[3,16,32]{1,0,2:T(4,128)S(1)}, f32[3,16,32]{1,0,2:T(4,128)S(1)}, u32[]{:S(2)}, u32[]{:S(2)}) collective-permute-start(f32[3,16,32]{1,0,2:T(4,128)S(1)} %get-tuple-element.53), channel_id=1, source_target_pairs={{0,28},{4,24},{8,20},{12,16},{16,12},{20,8},{24,4},{28,0},{1,29},{... | collective-permute-start | bytes 18440 | tf_op jit(solution)/shard_map/ppermute | solution.py:126
  79.2 28.0 %copy-start.4 = (f32[3,1,512]{2,1,0:T(1,128)S(1)}, f32[3,1,512]{2,1,0:T(1,128)}, u32[]{:S(2)}) copy-start(f32[3,1,512]{2,1,0:T(1,128)} %param.28) | copy-start | bytes 18436
  79.2 57.2 %copy-start.3 = (f32[3,1,512]{2,1,0:T(1,128)S(1)}, f32[3,1,512]{2,1,0:T(1,128)}, u32[]{:S(2)}) copy-start(f32[3,1,512]{2,1,0:T(1,128)} %param.26) | copy-start | bytes 18436
  87.6 8.9 %all-to-all-start.1 = ((f32[8,1,1536]{2,1,0:T(1,128)}), f32[8,1,1536]{2,1,0:T(1,128)S(1)}, u32[]{:S(2)}, u32[]{:S(2)}) async-start(f32[8,1,1536]{2,1,0:T(1,128)} %reshape.339), calls=%async_computation.1 | async-start | bytes 98304 | tf_op jit(solution)/shard_map/all_to_all | solution.py:163
  107.3 5.1 %collective-permute-start.7 = (f32[3,16]{1,0:T(4,128)S(1)}, f32[3,16]{1,0:T(4,128)S(1)}, u32[]{:S(2)}, u32[]{:S(2)}) collective-permute-start(f32[3,16]{1,0:T(4,128)S(1)} %get-tuple-element.84), channel_id=1, source_target_pairs={{0,4},{4,8},{8,12},{12,16},{16,20},{20,24},{24,28},{28,0},{1,5},{5... | collective-permute-start | bytes 584 | tf_op jit(solution)/shard_map/ppermute | solution.py:19
  107.4 10.7 %collective-permute-start.9 = (f32[3,16]{1,0:T(4,128)S(1)}, f32[3,16]{1,0:T(4,128)S(1)}, u32[]{:S(2)}, u32[]{:S(2)}) collective-permute-start(f32[3,16]{1,0:T(4,128)S(1)} %get-tuple-element.85), channel_id=1, source_target_pairs={{4,0},{8,4},{12,8},{16,12},{20,16},{24,20},{28,24},{0,28},{5,1},{9... | collective-permute-start | bytes 584 | tf_op jit(solution)/shard_map/ppermute | solution.py:22
  112.4 7.6 %collective-permute-start.8 = (f32[3,16]{1,0:T(4,128)S(1)}, f32[3,16]{1,0:T(4,128)S(1)}, u32[]{:S(2)}, u32[]{:S(2)}) collective-permute-start(f32[3,16]{1,0:T(4,128)S(1)} %collective-permute-done.7), channel_id=1, source_target_pairs={{0,1},{1,2},{2,3},{4,5},{5,6},{6,7},{8,9},{9,10},{10,11},{12,13},{... | collective-permute-start | bytes 584 | tf_op jit(solution)/shard_map/ppermute | solution.py:30
  118.1 4.9 %collective-permute-start.10 = (f32[3,16]{1,0:T(4,128)S(1)}, f32[3,16]{1,0:T(4,128)S(1)}, u32[]{:S(2)}, u32[]{:S(2)}) collective-permute-start(f32[3,16]{1,0:T(4,128)S(1)} %collective-permute-done.9), channel_id=1, source_target_pairs={{1,0},{2,1},{3,2},{5,4},{6,5},{7,6},{9,8},{10,9},{11,10},{13,12},{... | collective-permute-start | bytes 584 | tf_op jit(solution)/shard_map/ppermute | solution.py:30
  123.2 5.1 %collective-permute-start.11 = (f32[3,16]{1,0:T(4,128)S(1)}, f32[3,16]{1,0:T(4,128)S(1)}, u32[]{:S(2)}, u32[]{:S(2)}) collective-permute-start(f32[3,16]{1,0:T(4,128)S(1)} %get-tuple-element.82), channel_id=1, source_target_pairs={{0,4},{4,8},{8,12},{12,16},{16,20},{20,24},{24,28},{28,0},{1,5},{5... | collective-permute-start | bytes 584 | tf_op jit(solution)/shard_map/ppermute | solution.py:19
  123.2 8.2 %collective-permute-start.13 = (f32[3,16]{1,0:T(4,128)S(1)}, f32[3,16]{1,0:T(4,128)S(1)}, u32[]{:S(2)}, u32[]{:S(2)}) collective-permute-start(f32[3,16]{1,0:T(4,128)S(1)} %get-tuple-element.83), channel_id=1, source_target_pairs={{4,0},{8,4},{12,8},{16,12},{20,16},{24,20},{28,24},{0,28},{5,1},{9... | collective-permute-start | bytes 584 | tf_op jit(solution)/shard_map/ppermute | solution.py:22
  128.4 5.0 %collective-permute-start.12 = (f32[3,16]{1,0:T(4,128)S(1)}, f32[3,16]{1,0:T(4,128)S(1)}, u32[]{:S(2)}, u32[]{:S(2)}) collective-permute-start(f32[3,16]{1,0:T(4,128)S(1)} %collective-permute-done.11), channel_id=1, source_target_pairs={{0,1},{1,2},{2,3},{4,5},{5,6},{6,7},{8,9},{9,10},{10,11},{12,13},{... | collective-permute-start | bytes 584 | tf_op jit(solution)/shard_map/ppermute | solution.py:30
  131.5 4.9 %collective-permute-start.14 = (f32[3,16]{1,0:T(4,128)S(1)}, f32[3,16]{1,0:T(4,128)S(1)}, u32[]{:S(2)}, u32[]{:S(2)}) collective-permute-start(f32[3,16]{1,0:T(4,128)S(1)} %collective-permute-done.13), channel_id=1, source_target_pairs={{1,0},{2,1},{3,2},{5,4},{6,5},{7,6},{9,8},{10,9},{11,10},{13,12},{... | collective-permute-start | bytes 584 | tf_op jit(solution)/shard_map/ppermute | solution.py:30
  138.3 5.1 %collective-permute-start.15 = (f32[3,16,32]{1,0,2:T(4,128)S(1)}, f32[3,16,32]{1,0,2:T(4,128)S(1)}, u32[]{:S(2)}, u32[]{:S(2)}) collective-permute-start(f32[3,16,32]{1,0,2:T(4,128)S(1)} %get-tuple-element.51), channel_id=1, source_target_pairs={{0,4},{4,0},{8,12},{12,8},{16,20},{20,16},{24,28},{28,24},{1,5},{5... | collective-permute-start | bytes 18440 | tf_op jit(solution)/shard_map/ppermute | solution.py:126
  138.6 6.1 %collective-permute-start.16 = (f32[3,16,32]{1,0,2:T(4,128)S(1)}, f32[3,16,32]{1,0,2:T(4,128)S(1)}, u32[]{:S(2)}, u32[]{:S(2)}) collective-permute-start(f32[3,16,32]{1,0,2:T(4,128)S(1)} %get-tuple-element.50), channel_id=1, source_target_pairs={{0,8},{4,12},{8,0},{12,4},{16,24},{20,28},{24,16},{28,20},{1,9},{5... | collective-permute-start | bytes 18440 | tf_op jit(solution)/shard_map/ppermute | solution.py:126
  138.7 9.3 %collective-permute-start.17 = (f32[3,16,32]{1,0,2:T(4,128)S(1)}, f32[3,16,32]{1,0,2:T(4,128)S(1)}, u32[]{:S(2)}, u32[]{:S(2)}) collective-permute-start(f32[3,16,32]{1,0,2:T(4,128)S(1)} %get-tuple-element.49), channel_id=1, source_target_pairs={{0,12},{4,8},{8,4},{12,0},{16,28},{20,24},{24,20},{28,16},{1,13},{... | collective-permute-start | bytes 18440 | tf_op jit(solution)/shard_map/ppermute | solution.py:126
  141.3 9.7 %collective-permute-start.18 = (f32[3,16,32]{1,0,2:T(4,128)S(1)}, f32[3,16,32]{1,0,2:T(4,128)S(1)}, u32[]{:S(2)}, u32[]{:S(2)}) collective-permute-start(f32[3,16,32]{1,0,2:T(4,128)S(1)} %get-tuple-element.48), channel_id=1, source_target_pairs={{0,16},{4,20},{8,24},{12,28},{16,0},{20,4},{24,8},{28,12},{1,17},{... | collective-permute-start | bytes 18440 | tf_op jit(solution)/shard_map/ppermute | solution.py:126
  141.3 11.1 %collective-permute-start.19 = (f32[3,16,32]{1,0,2:T(4,128)S(1)}, f32[3,16,32]{1,0,2:T(4,128)S(1)}, u32[]{:S(2)}, u32[]{:S(2)}) collective-permute-start(f32[3,16,32]{1,0,2:T(4,128)S(1)} %get-tuple-element.47), channel_id=1, source_target_pairs={{0,20},{4,16},{8,28},{12,24},{16,4},{20,0},{24,12},{28,8},{1,21},{... | collective-permute-start | bytes 18440 | tf_op jit(solution)/shard_map/ppermute | solution.py:126
  143.4 9.0 %collective-permute-start.20 = (f32[3,16,32]{1,0,2:T(4,128)S(1)}, f32[3,16,32]{1,0,2:T(4,128)S(1)}, u32[]{:S(2)}, u32[]{:S(2)}) collective-permute-start(f32[3,16,32]{1,0,2:T(4,128)S(1)} %get-tuple-element.46), channel_id=1, source_target_pairs={{0,24},{4,28},{8,16},{12,20},{16,8},{20,12},{24,0},{28,4},{1,25},{... | collective-permute-start | bytes 18440 | tf_op jit(solution)/shard_map/ppermute | solution.py:126
  144.8 7.7 %collective-permute-start.21 = (f32[3,16,32]{1,0,2:T(4,128)S(1)}, f32[3,16,32]{1,0,2:T(4,128)S(1)}, u32[]{:S(2)}, u32[]{:S(2)}) collective-permute-start(f32[3,16,32]{1,0,2:T(4,128)S(1)} %get-tuple-element.45), channel_id=1, source_target_pairs={{0,28},{4,24},{8,20},{12,16},{16,12},{20,8},{24,4},{28,0},{1,29},{... | collective-permute-start | bytes 18440 | tf_op jit(solution)/shard_map/ppermute | solution.py:126
  208.4 5.1 %collective-permute-start.22 = (f32[3,16]{1,0:T(4,128)S(1)}, f32[3,16]{1,0:T(4,128)S(1)}, u32[]{:S(2)}, u32[]{:S(2)}) collective-permute-start(f32[3,16]{1,0:T(4,128)S(1)} %get-tuple-element.80), channel_id=1, source_target_pairs={{0,4},{4,8},{8,12},{12,16},{16,20},{20,24},{24,28},{28,0},{1,5},{5... | collective-permute-start | bytes 584 | tf_op jit(solution)/shard_map/ppermute | solution.py:19
  208.4 10.6 %collective-permute-start.24 = (f32[3,16]{1,0:T(4,128)S(1)}, f32[3,16]{1,0:T(4,128)S(1)}, u32[]{:S(2)}, u32[]{:S(2)}) collective-permute-start(f32[3,16]{1,0:T(4,128)S(1)} %get-tuple-element.81), channel_id=1, source_target_pairs={{4,0},{8,4},{12,8},{16,12},{20,16},{24,20},{28,24},{0,28},{5,1},{9... | collective-permute-start | bytes 584 | tf_op jit(solution)/shard_map/ppermute | solution.py:22
  213.5 7.4 %collective-permute-start.23 = (f32[3,16]{1,0:T(4,128)S(1)}, f32[3,16]{1,0:T(4,128)S(1)}, u32[]{:S(2)}, u32[]{:S(2)}) collective-permute-start(f32[3,16]{1,0:T(4,128)S(1)} %collective-permute-done.22), channel_id=1, source_target_pairs={{0,1},{1,2},{2,3},{4,5},{5,6},{6,7},{8,9},{9,10},{10,11},{12,13},{... | collective-permute-start | bytes 584 | tf_op jit(solution)/shard_map/ppermute | solution.py:30
  219.0 4.9 %collective-permute-start.25 = (f32[3,16]{1,0:T(4,128)S(1)}, f32[3,16]{1,0:T(4,128)S(1)}, u32[]{:S(2)}, u32[]{:S(2)}) collective-permute-start(f32[3,16]{1,0:T(4,128)S(1)} %collective-permute-done.24), channel_id=1, source_target_pairs={{1,0},{2,1},{3,2},{5,4},{6,5},{7,6},{9,8},{10,9},{11,10},{13,12},{... | collective-permute-start | bytes 584 | tf_op jit(solution)/shard_map/ppermute | solution.py:30
  224.2 5.1 %collective-permute-start.26 = (f32[3,16]{1,0:T(4,128)S(1)}, f32[3,16]{1,0:T(4,128)S(1)}, u32[]{:S(2)}, u32[]{:S(2)}) collective-permute-start(f32[3,16]{1,0:T(4,128)S(1)} %get-tuple-element.78), channel_id=1, source_target_pairs={{0,4},{4,8},{8,12},{12,16},{16,20},{20,24},{24,28},{28,0},{1,5},{5... | collective-permute-start | bytes 584 | tf_op jit(solution)/shard_map/ppermute | solution.py:19
  224.2 9.0 %collective-permute-start.28 = (f32[3,16]{1,0:T(4,128)S(1)}, f32[3,16]{1,0:T(4,128)S(1)}, u32[]{:S(2)}, u32[]{:S(2)}) collective-permute-start(f32[3,16]{1,0:T(4,128)S(1)} %get-tuple-element.79), channel_id=1, source_target_pairs={{4,0},{8,4},{12,8},{16,12},{20,16},{24,20},{28,24},{0,28},{5,1},{9... | collective-permute-start | bytes 584 | tf_op jit(solution)/shard_map/ppermute | solution.py:22
  229.3 5.8 %collective-permute-start.27 = (f32[3,16]{1,0:T(4,128)S(1)}, f32[3,16]{1,0:T(4,128)S(1)}, u32[]{:S(2)}, u32[]{:S(2)}) collective-permute-start(f32[3,16]{1,0:T(4,128)S(1)} %collective-permute-done.26), channel_id=1, source_target_pairs={{0,1},{1,2},{2,3},{4,5},{5,6},{6,7},{8,9},{9,10},{10,11},{12,13},{... | collective-permute-start | bytes 584 | tf_op jit(solution)/shard_map/ppermute | solution.py:30
  233.2 4.9 %collective-permute-start.29 = (f32[3,16]{1,0:T(4,128)S(1)}, f32[3,16]{1,0:T(4,128)S(1)}, u32[]{:S(2)}, u32[]{:S(2)}) collective-permute-start(f32[3,16]{1,0:T(4,128)S(1)} %collective-permute-done.28), channel_id=1, source_target_pairs={{1,0},{2,1},{3,2},{5,4},{6,5},{7,6},{9,8},{10,9},{11,10},{13,12},{... | collective-permute-start | bytes 584 | tf_op jit(solution)/shard_map/ppermute | solution.py:30
